TPU v7x, 128 devices: a whole 4x4x4 slice. The times are simulated.
128 devices in a mesh: cp: 8 (over x_hi, y), grp: 16 (over z, x_lo, core).
Axes of the slice: x: 4 (x_hi: 2, x_lo: 2; x = x_hi * 2 + x_lo), y: 4, z: 4, core: 2. Of those that a mesh axis runs over, the one named last changes fastest.
Arguments:
- queries: bfloat16 [32, 1024, 2048], P('grp', 'cp'), may hold values from -108 to 108
- keys: bfloat16 [32, 1024, 2048], P('grp', 'cp'), may hold values from -4 to 4
- values: bfloat16 [32, 1024, 2048], P('grp', 'cp'), may hold values from -6 to 6
- lengths: int32 [32], P('grp'), may hold values from 256 to 1024
- frame_map: bfloat16 [2048, 2176], replicated, may hold values from -0.125 to 0.125
- proj_weight: bfloat16 [2176, 4096], P('grp', 'cp'), may hold values from -0.125 to 0.125
- head_weight: bfloat16 [4096, 256], P('cp'), may hold values from -0.375 to 0.375
- act_embed: float32 [7, 4096], P(None, 'cp'), may hold values from -0.5 to 0.5
- actions: int32 [32, 7], P('grp'), may hold values from 0 to 255
- action_mask: int32 [32, 7], P('grp'), may hold values 0 or 1
- group_ids: int32 [32], P('grp'), may hold values from 0 to 3
- rewards: float32 [32], P('grp'), may hold values from -6 to 6
Outputs:
- logprobs: float32 [32, 7], P('grp')
- grad_proj: bfloat16 [2176, 4096], P('grp', 'cp')
- grad_head: bfloat16 [4096, 256], P('cp')
All inputs are finite; a program needn't handle non-finite values. No bound on the sum of `action_mask` on one device may be relied on, other than what follows from the above.
Results may differ from a plain program's by a relative error of at most 0.018.
Values may be sent and summed in bfloat16 or wider, within the bound.
No kernel may reach another device: no remote copies, remote signals or barrier semaphores. Data moves between devices by JAX's collectives and lax.ppermute only.
A program may use at most 128 MiB of HBM per device.

v0:
```python
import math
import jax
import jax.numpy as jnp
from jax import lax
from jax.sharding import PartitionSpec as P

HD = 128
SQRT_HALF = 0.7071067811865476
INV_ROOT_TAU = 0.3989422804014327
NEG_LARGE = -1e30


def in_order(parts, dim):
    parts = jnp.moveaxis(parts, 0, dim)
    shape = parts.shape
    return parts.reshape(*shape[:dim], shape[dim] * shape[dim + 1], *shape[dim + 2 :])


def copy_for_each(array, axis):
    copies = jnp.broadcast_to(array, (lax.axis_size(axis), *array.shape))
    return lax.all_to_all(copies, axis, split_axis=0, concat_axis=0, tiled=True)


def gathered_copies(array, axis, dim):
    return in_order(copy_for_each(array, axis), dim)


def taken_together(array, axis):
    return copy_for_each(array, axis).sum(axis=0)


def together(arrays, axis):
    ravelled, at, outs = (jnp.concatenate([a.reshape(-1) for a in arrays]), 0, [])
    subtotal = taken_together(ravelled, axis)
    for a in arrays:
        outs.append(subtotal[at : at + a.size].reshape(a.shape))
        at += a.size
    return tuple(outs)


def total_of_pieces(array, axis):
    parts = lax.all_gather(array, axis).astype(jnp.float32)
    return parts.sum(axis=0)


def cut_along(array, dim, count):
    before, after = (array.shape[:dim], array.shape[dim + 1 :])
    return jnp.moveaxis(array.reshape(*before, count, -1, *after), dim, 0)


def sent_and_summed(array, axis, dim):
    count = lax.axis_size(axis)
    parts = lax.all_to_all(cut_along(array, dim, count), axis, 0, 0, tiled=True)
    return jnp.sum(parts.astype(jnp.float32), axis=0)


def gelu_exact(values_in):
    return 0.5 * values_in * (1.0 + lax.erf(values_in * SQRT_HALF))


def gelu_slope(values_in):
    return (
        0.5 * (1.0 + lax.erf(values_in * SQRT_HALF))
        + values_in * jnp.exp(-0.5 * values_in * values_in) * INV_ROOT_TAU
    )


def fetch_columns(proj_weight):
    return gathered_copies(proj_weight, "grp", 0)


def attention(queries, keys, values, lengths):
    episodes_here, tokens_here, att_width = queries.shape
    head_count = att_width // HD
    query_heads = queries.reshape(episodes_here, tokens_here, head_count, HD)
    key_heads = keys.reshape(episodes_here, tokens_here, head_count, HD)
    value_heads = values.reshape(episodes_here, tokens_here, head_count, HD)
    query_all, key_all, value_all = (
        lax.all_to_all(query_heads, "cp", split_axis=2, concat_axis=1, tiled=True),
        lax.all_to_all(key_heads, "cp", split_axis=2, concat_axis=1, tiled=True),
        lax.all_to_all(value_heads, "cp", split_axis=2, concat_axis=1, tiled=True),
    )
    seq_span = query_all.shape[1]
    scores = jnp.einsum(
        "eihd,ejhd->ehij", query_all, key_all, preferred_element_type=jnp.float32
    ) / math.sqrt(HD)
    live_keys = (jnp.arange(seq_span, dtype=jnp.int32)[None, :] < lengths[:, None])[
        :, None, None, :
    ]
    scores = jnp.where(live_keys, scores, NEG_LARGE)
    row_max = jnp.max(scores, axis=-1, keepdims=True)
    probs = jnp.where(live_keys, jnp.exp(scores - row_max), 0.0)
    row_total = jnp.sum(probs, axis=-1)
    weighted = jnp.einsum(
        "ehij,ejhd->eihd", probs.astype(jnp.bfloat16), value_all, preferred_element_type=jnp.float32
    )
    output = (weighted / jnp.transpose(row_total, (0, 2, 1))[..., None]).astype(jnp.bfloat16)
    returned = lax.all_to_all(output, "cp", split_axis=1, concat_axis=2, tiled=True)
    return returned.reshape(episodes_here, tokens_here, att_width)


def per_device(
    queries,
    keys,
    values,
    lengths,
    frame_map,
    proj_weight,
    head_weight,
    act_embed,
    actions,
    action_mask,
    group_ids,
    rewards,
):
    episodes_here, tokens_here, att_width = queries.shape
    action_count = act_embed.shape[0]
    lengths_real = lengths.astype(jnp.float32)
    attended = attention(queries, keys, values, lengths)
    proj_cols = fetch_columns(proj_weight)
    frames = jnp.dot(
        attended.reshape(episodes_here * tokens_here, att_width),
        frame_map,
        preferred_element_type=jnp.float32,
    )
    frames = frames.astype(jnp.bfloat16).reshape(episodes_here, tokens_here, frame_map.shape[1])
    all_frames = lax.all_gather(frames, "cp", axis=1, tiled=True)
    seq_span = all_frames.shape[1]
    flat_frames = all_frames.reshape(episodes_here * seq_span, all_frames.shape[2])
    col_count = proj_cols.shape[1]
    pre_act = jnp.dot(flat_frames, proj_cols, preferred_element_type=jnp.float32).reshape(
        episodes_here, seq_span, col_count
    )
    hidden = gelu_exact(pre_act)
    token_mask = (jnp.arange(seq_span, dtype=jnp.int32)[None, :] < lengths[:, None]).astype(
        jnp.float32
    )
    pooled = jnp.sum(token_mask[:, :, None] * hidden, axis=1) / lengths_real[:, None]
    sum_input = pooled[:, None, :] + act_embed[None, :, :]
    head_input = sum_input.astype(jnp.bfloat16).reshape(episodes_here * action_count, col_count)
    partial_logits = jnp.dot(head_input, head_weight, preferred_element_type=jnp.float32)
    episodes_total = episodes_here * lax.axis_size("grp")
    group_count = max(1, episodes_total // 8)
    membership = (group_ids[:, None] == jnp.arange(group_count, dtype=jnp.int32)[None, :]).astype(
        jnp.float32
    )
    masked = action_mask.astype(jnp.float32)
    logits = taken_together(partial_logits, "cp")
    reward_sums, squares, group_sizes, mask_total = together(
        (
            jnp.sum(membership * rewards[:, None], axis=0),
            jnp.sum(membership * (rewards * rewards)[:, None], axis=0),
            jnp.sum(membership, axis=0),
            jnp.sum(masked),
        ),
        "grp",
    )
    log_all = jax.nn.log_softmax(logits, axis=-1)
    bin_ids = jnp.arange(head_weight.shape[1], dtype=jnp.int32)
    picked = (actions.reshape(-1)[:, None] == bin_ids[None, :]).astype(jnp.float32)
    logprobs = jnp.sum(picked * log_all, axis=-1).reshape(episodes_here, action_count)
    size_floor = jnp.maximum(group_sizes, 1.0)
    group_mean = reward_sums / size_floor
    variance = squares / size_floor - group_mean * group_mean
    group_scale = jnp.sqrt(jnp.maximum(variance, 1.0))
    advantage = (rewards - jnp.sum(membership * group_mean[None, :], axis=1)) / jnp.sum(
        membership * group_scale[None, :], axis=1
    )
    loss_weight = (-masked * advantage[:, None] / jnp.maximum(mask_total, 1.0)).reshape(-1)
    logit_grad = (loss_weight[:, None] * (picked - jnp.exp(log_all))).astype(jnp.bfloat16)
    head_term = lax.dot_general(
        head_input, logit_grad, (((0,), (0,)), ((), ())), preferred_element_type=jnp.float32
    )
    grad_head = (
        total_of_pieces(head_term.astype(jnp.bfloat16), "grp")
        .astype(jnp.float32)
        .astype(jnp.bfloat16)
    )
    pull_back = lax.dot_general(
        logit_grad, head_weight, (((1,), (1,)), ((), ())), preferred_element_type=jnp.float32
    )
    pool_grad = jnp.sum(pull_back.reshape(episodes_here, action_count, col_count), axis=1)
    scaled_mask = token_mask / lengths_real[:, None]
    act_grad = (scaled_mask[:, :, None] * pool_grad[:, None, :] * gelu_slope(pre_act)).astype(
        jnp.bfloat16
    )
    act_flat = act_grad.reshape(episodes_here * seq_span, col_count)
    grad_proj = sent_and_summed(
        lax.dot_general(
            flat_frames, act_flat, (((0,), (0,)), ((), ())), preferred_element_type=jnp.float32
        ).astype(jnp.bfloat16),
        "grp",
        0,
    ).astype(jnp.bfloat16)
    return (logprobs, grad_proj, grad_head)


def solution(mesh):
    in_specs = (
        P("grp", "cp", None),
        P("grp", "cp", None),
        P("grp", "cp", None),
        P("grp"),
        P(),
        P("grp", "cp"),
        P("cp", None),
        P(None, "cp"),
        P("grp", None),
        P("grp", None),
        P("grp"),
        P("grp"),
    )
    out_specs = (P("grp", None), P("grp", "cp"), P("cp", None))
    return jax.shard_map(
        per_device, mesh=mesh, in_specs=in_specs, out_specs=out_specs, check_vma=False
    )
```

profile of v0, /device:TPU:1, one launch (start us, length us, event | category | flops | bytes accessed | tf_op | source)
XLA Modules:
  0.0 328.7 jit_solution(10078888517784571058)
XLA Ops:
  7.2 1.7 copy.85
  8.9 1.1 copy.86
  10.0 7.5 %all-to-all-start = ((bf16[2,128,16,128]{1,3,0,2:T(8,128)(2,1)}), bf16[2,128,16,128]{1,3,0,2:T(8,128)(2,1)S(1)}, u32[]{:S(2)}, u32[]{:S(2)}) async-start(bf16[2,128,16,128]{1,3,0,2:T(8,128)(2,1)} %copy.86), calls=%async_computation | async-start | bytes 2097152 | tf_op jit(solution)/shard_map/all_to_all | solution.py:79
  17.4 0.7 copy.89
  18.1 1.1 copy.90
  19.2 12.5 %all-to-all-done = bf16[2,128,16,128]{1,3,0,2:T(8,128)(2,1)S(1)} async-done(((bf16[2,128,16,128]{1,3,0,2:T(8,128)(2,1)}), bf16[2,128,16,128]{1,3,0,2:T(8,128)(2,1)S(1)}, u32[]{:S(2)}, u32[]{:S(2)}) %all-to-all-start) | async-done | bytes 1048608 | tf_op jit(solution)/shard_map/all_to_all | solution.py:79
  31.7 5.9 %all-to-all-start.1 = ((bf16[2,128,16,128]{1,3,0,2:T(8,128)(2,1)}), bf16[2,128,16,128]{1,3,0,2:T(8,128)(2,1)S(1)}, u32[]{:S(2)}, u32[]{:S(2)}) async-start(bf16[2,128,16,128]{1,3,0,2:T(8,128)(2,1)} %copy.90), calls=%async_computation.1 | async-start | bytes 2097152 | tf_op jit(solution)/shard_map/all_to_all | solution.py:80
  37.6 1.6 copy.93
  39.2 1.1 copy.94
  40.2 11.7 %all-to-all-done.1 = bf16[2,128,16,128]{1,3,0,2:T(8,128)(2,1)S(1)} async-done(((bf16[2,128,16,128]{1,3,0,2:T(8,128)(2,1)}), bf16[2,128,16,128]{1,3,0,2:T(8,128)(2,1)S(1)}, u32[]{:S(2)}, u32[]{:S(2)}) %all-to-all-start.1) | async-done | bytes 1048608 | tf_op jit(solution)/shard_map/all_to_all | solution.py:80
  52.0 5.7 %all-to-all-start.2 = ((bf16[2,128,16,128]{1,3,0,2:T(8,128)(2,1)}), bf16[2,128,16,128]{1,3,0,2:T(8,128)(2,1)S(1)}, u32[]{:S(2)}, u32[]{:S(2)}) async-start(bf16[2,128,16,128]{1,3,0,2:T(8,128)(2,1)} %copy.94), calls=%async_computation.2 | async-start | bytes 2097152 | tf_op jit(solution)/shard_map/all_to_all | solution.py:81
  57.8 1.3 copy.88
  59.1 1.4 copy.92
  60.5 11.6 %all-to-all-done.2 = bf16[2,128,16,128]{1,3,0,2:T(8,128)(2,1)S(1)} async-done(((bf16[2,128,16,128]{1,3,0,2:T(8,128)(2,1)}), bf16[2,128,16,128]{1,3,0,2:T(8,128)(2,1)S(1)}, u32[]{:S(2)}, u32[]{:S(2)}) %all-to-all-start.2) | async-done | bytes 1048608 | tf_op jit(solution)/shard_map/all_to_all | solution.py:81
  72.1 0.7 copy.96
  72.8 11.3 %fusion.32 = (f32[2,2,1024]{2,1,0:T(2,128)S(1)}, bf16[2,2,1024,1024]{2,3,1,0:T(8,128)(2,1)}) fusion(pred[2,1024]{1,0:T(4,128)(4,1)S(1)} %get-tuple-element.11, bf16[2,1024,2,128]{3,1,2,0:T(8,128)(2,1)S(1)} %bitcast.63, bf16[2,1024,2,128]{3,1,2,0:T(8,128)(2,1)} %bitcast.64), kind=kOutput, calls=%fused_computation.59 | convolution fusion | flops 1098908672 | bytes 10504192 | tf_op jit(solution)/shard_map/sub | solution.py:92
  84.0 6.3 %fusion.15 = bf16[2,1024,2,128]{3,1,2,0:T(8,128)(2,1)S(1)} fusion(bf16[2,1024,2,128]{3,1,2,0:T(8,128)(2,1)S(1)} %bitcast.65, bf16[2,2,1024,1024]{2,3,1,0:T(8,128)(2,1)} %get-tuple-element.13, f32[2,1024,2]{1,2,0:T(2,128)S(1)} %bitcast.66), kind=kOutput, calls=%fused_computation.22 | convolution fusion | flops 1074790400 | bytes 10502144 | tf_op jit(solution)/shard_map/ehij,ejhd->eihd/dot_general | solution.py:94
  90.4 1.1 copy.98
  91.5 21.2 %all_to_all.90 = bf16[2,1024,2,128]{3,2,0,1:T(2,128)(2,1)S(1)} all-to-all(bf16[2,1024,2,128]{3,2,0,1:T(2,128)(2,1)S(1)} %copy.98), channel_id=1, replica_groups=mesh['cp'=8,'grp'=16] {'cp'}, dimensions={1} | all-to-all | bytes 2097152 | tf_op jit(solution)/shard_map/all_to_all | solution.py:98
  112.6 0.7 copy.116
  113.3 0.8 reshape_reshape.3
  114.2 7.2 %convolution_convert_fusion = bf16[256,2176]{1,0:T(8,128)(2,1)} fusion(bf16[256,2048]{1,0:T(8,128)(2,1)S(1)} %reshape_reshape.3, bf16[2048,2176]{1,0:T(8,128)(2,1)} %param.16), kind=kOutput, calls=%fused_computation.20 | convolution fusion | flops 2282258432 | bytes 11075584 | tf_op jit(solution)/shard_map/dot_general | solution.py:121
  121.4 0.6 convert_reduce_fusion.1
  122.1 0.1 select_reduce_fusion.4
  122.1 0.7 pad_maximum_fusion
  122.9 13.2 %all_to_all.91 = f32[16,1,13]{2,1,0:T(1,128)S(1)} all-to-all(f32[16,1,13]{2,1,0:T(1,128)S(1)} %broadcast_in_dim.33), channel_id=1, replica_groups=mesh['cp'=8,'grp'=16] {'grp'}, dimensions={0} | all-to-all | bytes 1664 | tf_op jit(solution)/shard_map/all_to_all | solution.py:21
  136.1 1.6 broadcast_in_dim.31
  137.6 4.2 %all-to-all-start.4 = ((bf16[16,136,512]{2,1,0:T(8,128)(2,1)}), bf16[16,136,512]{2,1,0:T(8,128)(2,1)S(1)}, u32[]{:S(2)}, u32[]{:S(2)}) async-start(bf16[16,136,512]{2,1,0:T(8,128)(2,1)} %broadcast_in_dim.31), calls=%async_computation.4 | async-start | bytes 4456448 | tf_op jit(solution)/shard_map/all_to_all | solution.py:21
  141.9 0.6 slice.15
  143.3 0.2 select_reduce_fusion.2
  143.5 30.1 %all-to-all-done.4 = bf16[16,136,512]{2,1,0:T(8,128)(2,1)S(1)} async-done(((bf16[16,136,512]{2,1,0:T(8,128)(2,1)}), bf16[16,136,512]{2,1,0:T(8,128)(2,1)S(1)}, u32[]{:S(2)}, u32[]{:S(2)}) %all-to-all-start.4) | async-done | bytes 2228256 | tf_op jit(solution)/shard_map/all_to_all | solution.py:21
  173.6 63.3 %all-gather.4.cloned.1.call-done = bf16[2,1024,2176]{2,1,0:T(8,128)(2,1)} async-done(((bf16[2,128,2176]{2,1,0:T(8,128)(2,1)}), bf16[2,1024,2176]{2,1,0:T(8,128)(2,1)}) %all-gather.4.cloned.1.call-update) | async-done | bytes 8912912 | tf_op jit(solution)/shard_map/all_gather | solution.py:127
  236.9 9.1 %multiply_reduce_fusion = (f32[2,512]{1,0:T(2,128)S(1)}, f32[2,1024,512]{2,1,0:T(8,128)}) fusion(f32[2,1024]{1,0:T(2,128)S(1)} %get-tuple-element.10, bf16[2,1024,2176]{2,1,0:T(8,128)(2,1)} %all-gather.4.cloned.1.call-done, bf16[2176,512,1]{1,0,2:T(8,128)(2,1)S(1)} %bitcast.60), kind=kOutput, calls=%fused_computation.18 | convolution fusion | flops 4569693184 | bytes 15347712 | tf_op jit(solution)/shard_map/dot_general | solution.py:131
  246.1 0.1 fusion.33
  246.3 0.7 broadcast_in_dim.32
  247.0 3.4 %all-to-all-start.5 = ((f32[8,14,256]{2,1,0:T(8,128)}), f32[8,14,256]{2,1,0:T(8,128)S(1)}, u32[]{:S(2)}, u32[]{:S(2)}) async-start(f32[8,14,256]{2,1,0:T(8,128)} %broadcast_in_dim.32), calls=%async_computation.5 | async-start | bytes 262144 | tf_op jit(solution)/shard_map/all_to_all | solution.py:21
  250.5 6.7 %all-to-all-done.5 = f32[8,14,256]{2,1,0:T(8,128)S(1)} async-done(((f32[8,14,256]{2,1,0:T(8,128)}), f32[8,14,256]{2,1,0:T(8,128)S(1)}, u32[]{:S(2)}, u32[]{:S(2)}) %all-to-all-start.5) | async-done | bytes 114720 | tf_op jit(solution)/shard_map/all_to_all | solution.py:21
  257.2 0.1 reduce_max.20
  257.3 0.2 exponential_reduce_fusion
  257.5 1.0 convolution_convert_fusion.1
  258.6 0.2 fusion.31
  258.9 11.9 %fusion.7 = bf16[2176,512]{1,0:T(8,128)(2,1)} fusion(bf16[2,1024,2176]{2,1,0:T(8,128)(2,1)} %all-gather.4.cloned.1.call-done, f32[2,1024,512]{2,1,0:T(8,128)} %get-tuple-element.15, f32[2,512]{1,0:T(2,128)S(1)} %reduce_sum.154, f32[2,1024]{1,0:T(2,128)S(1)} %broadcast_divide_fusion), kind=kOutput, calls=%fused_computation.11 | convolution fusion | flops 4576051200 | bytes 15347712 | tf_op jit(solution)/shard_map/dot_general | solution.py:189
  270.8 6.8 %all-to-all-start.7 = ((bf16[16,136,512]{2,1,0:T(8,128)(2,1)}), bf16[16,136,512]{2,1,0:T(8,128)(2,1)S(1)}, u32[]{:S(2)}, u32[]{:S(2)}) async-start(bf16[16,136,512]{2,1,0:T(8,128)(2,1)} %bitcast.61), calls=%async_computation.7 | async-start | bytes 4456448 | tf_op jit(solution)/shard_map/all_to_all | solution.py:53
  277.6 0.2 select_reduce_fusion
  277.7 0.6 reshape.155
  278.4 38.9 %all-to-all-done.7 = bf16[16,136,512]{2,1,0:T(8,128)(2,1)S(1)} async-done(((bf16[16,136,512]{2,1,0:T(8,128)(2,1)}), bf16[16,136,512]{2,1,0:T(8,128)(2,1)S(1)}, u32[]{:S(2)}, u32[]{:S(2)}) %all-to-all-start.7) | async-done | bytes 2228256 | tf_op jit(solution)/shard_map/all_to_all | solution.py:53
  317.3 1.0 reduce_sum.155
  318.3 3.5 %reduce_sum.156 = bf16[512,256]{1,0:T(8,128)(2,1)} reduce(bf16[16,512,256]{2,1,0:T(8,128)(2,1)} %bitcast.51, bf16[]{:T(256)} %constant.36.clone.1), dimensions={0}, to_apply=%region_16.17 | reduce | flops 1966080 | bytes 4456450 | tf_op jit(solution)/shard_map/reduce_sum | solution.py:43
  (43 shorter events, 0.8 us)
Async XLA Ops:
  7.2 239.0 %copy-start = (bf16[512,256]{1,0:T(8,128)(2,1)S(1)}, bf16[512,256]{1,0:T(8,128)(2,1)}, u32[]{:S(2)}) copy-start(bf16[512,256]{1,0:T(8,128)(2,1)} %param.18) | copy-start | bytes 786436
  7.2 10.3 %copy-start.1 = (bf16[2,128,2048]{2,1,0:T(8,128)(2,1)S(1)}, bf16[2,128,2048]{2,1,0:T(8,128)(2,1)}, u32[]{:S(2)}) copy-start(bf16[2,128,2048]{2,1,0:T(8,128)(2,1)} %param.13) | copy-start | bytes 3145732
  10.0 21.7 %all-to-all-start = ((bf16[2,128,16,128]{1,3,0,2:T(8,128)(2,1)}), bf16[2,128,16,128]{1,3,0,2:T(8,128)(2,1)S(1)}, u32[]{:S(2)}, u32[]{:S(2)}) async-start(bf16[2,128,16,128]{1,3,0,2:T(8,128)(2,1)} %copy.86), calls=%async_computation | async-start | bytes 2097152 | tf_op jit(solution)/shard_map/all_to_all | solution.py:79
  19.2 38.5 %copy-start.5 = (s32[2]{0:T(128)S(1)}, s32[2]{0:T(128)}, u32[]{:S(2)}) copy-start(s32[2]{0:T(128)} %param.15) | copy-start | bytes 28
  31.7 20.3 %all-to-all-start.1 = ((bf16[2,128,16,128]{1,3,0,2:T(8,128)(2,1)}), bf16[2,128,16,128]{1,3,0,2:T(8,128)(2,1)S(1)}, u32[]{:S(2)}, u32[]{:S(2)}) async-start(bf16[2,128,16,128]{1,3,0,2:T(8,128)(2,1)} %copy.90), calls=%async_computation.1 | async-start | bytes 2097152 | tf_op jit(solution)/shard_map/all_to_all | solution.py:80
  52.0 20.1 %all-to-all-start.2 = ((bf16[2,128,16,128]{1,3,0,2:T(8,128)(2,1)}), bf16[2,128,16,128]{1,3,0,2:T(8,128)(2,1)S(1)}, u32[]{:S(2)}, u32[]{:S(2)}) async-start(bf16[2,128,16,128]{1,3,0,2:T(8,128)(2,1)} %copy.94), calls=%async_computation.2 | async-start | bytes 2097152 | tf_op jit(solution)/shard_map/all_to_all | solution.py:81
  57.7 179.2 %all-gather.4.cloned.1.call-start = ((), (), s32[]{:S(2)}) async-start(), calls=%async_computation.8 | async-start | bytes 10027008 | tf_op jit(solution)/shard_map/all_gather | solution.py:127
  59.1 13.6 %copy-start.2 = (bf16[2,8,128,2,128]{4,2,1,3,0:T(8,128)(2,1)S(1)}, bf16[2,8,128,2,128]{4,2,1,3,0:T(8,128)(2,1)}, u32[]{:S(2)}) copy-start(bf16[2,8,128,2,128]{4,2,1,3,0:T(8,128)(2,1)} %copy.88) | copy-start | bytes 3145732
  114.2 7.3 %copy-start.7 = (f32[2]{0:T(128)S(1)}, f32[2]{0:T(128)}, u32[]{:S(2)}) copy-start(f32[2]{0:T(128)} %param.23) | copy-start | bytes 28
  114.2 7.3 %copy-start.8 = (s32[2,7]{1,0:T(2,128)S(1)}, s32[2,7]{1,0:T(2,128)}, u32[]{:S(2)}) copy-start(s32[2,7]{1,0:T(2,128)} %param.21) | copy-start | bytes 172
  114.2 7.9 %copy-start.6 = (s32[2]{0:T(128)S(1)}, s32[2]{0:T(128)}, u32[]{:S(2)}) copy-start(s32[2]{0:T(128)} %param.22) | copy-start | bytes 28
  114.2 21.9 %copy-start.3 = (bf16[136,512]{1,0:T(8,128)(2,1)S(1)}, bf16[136,512]{1,0:T(8,128)(2,1)}, u32[]{:S(2)}) copy-start(bf16[136,512]{1,0:T(8,128)(2,1)} %param.17) | copy-start | bytes 417796
  121.4 20.4 %copy-start.9 = (s32[2,7]{1,0:T(2,128)S(1)}, s32[2,7]{1,0:T(2,128)}, u32[]{:S(2)}) copy-start(s32[2,7]{1,0:T(2,128)} %param.20) | copy-start | bytes 172
  137.6 36.0 %all-to-all-start.4 = ((bf16[16,136,512]{2,1,0:T(8,128)(2,1)}), bf16[16,136,512]{2,1,0:T(8,128)(2,1)S(1)}, u32[]{:S(2)}, u32[]{:S(2)}) async-start(bf16[16,136,512]{2,1,0:T(8,128)(2,1)} %broadcast_in_dim.31), calls=%async_computation.4 | async-start | bytes 4456448 | tf_op jit(solution)/shard_map/all_to_all | solution.py:21
  236.9 9.2 %copy-start.4 = (f32[7,512]{1,0:T(8,128)S(1)}, f32[7,512]{1,0:T(8,128)}, u32[]{:S(2)}) copy-start(f32[7,512]{1,0:T(8,128)} %param.19) | copy-start | bytes 43012
  247.0 10.3 %all-to-all-start.5 = ((f32[8,14,256]{2,1,0:T(8,128)}), f32[8,14,256]{2,1,0:T(8,128)S(1)}, u32[]{:S(2)}, u32[]{:S(2)}) async-start(f32[8,14,256]{2,1,0:T(8,128)} %broadcast_in_dim.32), calls=%async_computation.5 | async-start | bytes 262144 | tf_op jit(solution)/shard_map/all_to_all | solution.py:21
  250.3 67.9 %all-gather.6.cloned.1.call-start = ((), (), s32[]{:S(2)}) async-start(), calls=%async_computation.9 | async-start | bytes 4456448 | tf_op jit(solution)/shard_map/all_gather | solution.py:42
  270.8 46.5 %all-to-all-start.7 = ((bf16[16,136,512]{2,1,0:T(8,128)(2,1)}), bf16[16,136,512]{2,1,0:T(8,128)(2,1)S(1)}, u32[]{:S(2)}, u32[]{:S(2)}) async-start(bf16[16,136,512]{2,1,0:T(8,128)(2,1)} %bitcast.61), calls=%async_computation.7 | async-start | bytes 4456448 | tf_op jit(solution)/shard_map/all_to_all | solution.py:53
Sparse Core Ops, SparseCore 0:
  121.5 115.2 all-gather.3
  258.7 59.1 all-gather.5
where the time goes:
time: 329 us
  waiting for transfers between devices  175 us (53%)
  matrix products  47.1 us (14%)
  blocking collectives  34.3 us (10%)
  starting transfers between devices  33.5 us (10%)
  local copies, waits for them, and re-layouts  16.9 us (5%)
  between operations  14.9 us (5%)
  other arithmetic  7.1 us (2%)
    all_gather x1, waiting for transfers between devices, per_device(): all_frames = lax.all_gather(frames, 'cp', axis=1, tiled=True)  63.3 us
    all_to_all x1, waiting for transfers between devices, sent_and_summed(): parts = lax.all_to_all(cut_along(array, dim, count), axis, 0, 0, tiled=True)  38.9 us
    all_to_all x2, waiting for transfers between devices, copy_for_each(): return lax.all_to_all(copies, axis, split_axis=0, concat_axis=0, tiled=True)  36.8 us
    all_to_all x1, blocking collectives, attention(): lax.all_to_all(output, 'cp', split_axis=1, concat_axis=2, tiled=True)  21.2 us
    all_to_all x1, blocking collectives, copy_for_each(): return lax.all_to_all(copies, axis, split_axis=0, concat_axis=0, tiled=True)  13.2 us
    all_to_all x1, waiting for transfers between devices, attention(): lax.all_to_all(query_heads, 'cp', split_axis=2, concat_axis=1, tiled=True)  12.5 us
    dot_general x1, matrix products, per_device(): lax.dot_general(flat_frames, act_flat, (((0,), (0,)), ((), ())), preferre...  11.9 us
    all_to_all x1, waiting for transfers between devices, attention(): lax.all_to_all(key_heads, 'cp', split_axis=2, concat_axis=1, tiled=True)  11.7 us
  transfers between devices with their start and end apart: 8, of which 7 were waited for; matrix products, arithmetic and copies ran while one was open for 8% of the time, Pallas kernels for 0%

commit v1 on v0

--- a/solution.py
+++ b/solution.py
@@ -124,7 +124,9 @@
         preferred_element_type=jnp.float32,
     )
     frames = frames.astype(jnp.bfloat16).reshape(episodes_here, tokens_here, frame_map.shape[1])
-    all_frames = lax.all_gather(frames, "cp", axis=1, tiled=True)
+    all_frames = jnp.concatenate(
+        lax.all_to_all(jnp.stack([frames] * lax.axis_size("cp")), "cp", 0, 0), axis=1
+    )
     seq_span = all_frames.shape[1]
     flat_frames = all_frames.reshape(episodes_here * seq_span, all_frames.shape[2])
     col_count = proj_cols.shape[1]

time: 329 us -> 364 us (1.11)
  blocking collectives: 34.3 us -> 105 us
  waiting for transfers between devices: 175 us -> 112 us
  starting transfers between devices: 33.5 us -> 48.3 us
  local copies, waits for them, and re-layouts: 16.9 us -> 27.6 us
  other arithmetic: 7.1 us -> 11.1 us
    all_to_all x2 -> x1, blocking collectives: 34.3 us -> 105 us  [per_device(): lax.all_to_all(jnp.stack([frames] * lax.axis_size('cp')), 'cp', 0, 0)]
    all_gather x1 -> x0, waiting for transfers between devices: 63.3 us -> none  [per_device(): all_frames = lax.all_gather(frames, 'cp', axis=1, tiled=True)]
    all_to_all x0 -> x1, waiting for transfers between devices: none -> 13 us  [attention(): lax.all_to_all(output, 'cp', split_axis=1, concat_axis=2, tiled=True)]
    all_to_all x2 -> x3, waiting for transfers between devices: 36.8 us -> 25.4 us  [copy_for_each(): return lax.all_to_all(copies, axis, split_axis=0, concat_axis=0, tiled=True)]
    all_to_all x2 -> x3, starting transfers between devices: 7.55 us -> 17.8 us  [copy_for_each(): return lax.all_to_all(copies, axis, split_axis=0, concat_axis=0, tiled=True)]
    all_to_all x0 -> x1, local copies, waits for them, and re-layouts: none -> 7.97 us  [per_device(): lax.all_to_all(jnp.stack([frames] * lax.axis_size('cp')), 'cp', 0, 0)]
    all_to_all x0 -> x1, starting transfers between devices: none -> 5.7 us  [attention(): lax.all_to_all(output, 'cp', split_axis=1, concat_axis=2, tiled=True)]
    convert_element_type x0 -> x1, other arithmetic: none -> 4.01 us  [per_device(): (scaled_mask[:, :, None] * pool_grad[:, None, :] * gelu_slope(pre_act)).a...]
  transfers between devices with their start and end apart: 8 -> 9, of which waited for: 7 -> 7; matrix products, arithmetic and copies ran while one was open for 8% -> 11% of each run, Pallas kernels for 0% -> 0%
where the time goes in v1:
time: 364 us; the launch traced here: 363 us
  waiting for transfers between devices  112 us (31%)
  blocking collectives  105 us (29%)
  starting transfers between devices  48.3 us (13%)
  matrix products  44.1 us (12%)
  local copies, waits for them, and re-layouts  27.6 us (8%)
  between operations  14.9 us (4%)
  other arithmetic  11.1 us (3%)
    all_to_all x1, blocking collectives, per_device(): lax.all_to_all(jnp.stack([frames] * lax.axis_size('cp')), 'cp', 0, 0)  105 us
    all_to_all x1, waiting for transfers between devices, sent_and_summed(): parts = lax.all_to_all(cut_along(array, dim, count), axis, 0, 0, tiled=True)  37.6 us
    all_to_all x3, waiting for transfers between devices, copy_for_each(): return lax.all_to_all(copies, axis, split_axis=0, concat_axis=0, tiled=True)  25.4 us
    all_to_all x3, starting transfers between devices, copy_for_each(): return lax.all_to_all(copies, axis, split_axis=0, concat_axis=0, tiled=True)  17.8 us
    all_to_all x1, waiting for transfers between devices, attention(): lax.all_to_all(output, 'cp', split_axis=1, concat_axis=2, tiled=True)  13 us
    all_to_all x1, waiting for transfers between devices, attention(): lax.all_to_all(value_heads, 'cp', split_axis=2, concat_axis=1, tiled=True)  12.5 us
    all_to_all x1, waiting for transfers between devices, attention(): lax.all_to_all(query_heads, 'cp', split_axis=2, concat_axis=1, tiled=True)  11.7 us
    all_to_all x1, waiting for transfers between devices, attention(): lax.all_to_all(key_heads, 'cp', split_axis=2, concat_axis=1, tiled=True)  11.7 us
  transfers between devices with their start and end apart: 9, of which 7 were waited for; matrix products, arithmetic and copies ran while one was open for 11% of the time, Pallas kernels for 0%

profile of v1, /device:TPU:1, one launch (start us, length us, event | category | flops | bytes accessed | tf_op | source)
XLA Modules:
  0.0 362.6 jit_solution(9954154206239685788)
XLA Ops:
  7.2 1.7 copy.106
  8.9 1.1 copy.107
  10.0 7.5 %all-to-all-start.2 = ((bf16[2,128,16,128]{1,3,0,2:T(8,128)(2,1)}), bf16[2,128,16,128]{1,3,0,2:T(8,128)(2,1)S(1)}, u32[]{:S(2)}, u32[]{:S(2)}) async-start(bf16[2,128,16,128]{1,3,0,2:T(8,128)(2,1)} %copy.107), calls=%async_computation.2 | async-start | bytes 2097152 | tf_op jit(solution)/shard_map/all_to_all | solution.py:81
  17.4 0.7 copy.98
  18.1 1.1 copy.99
  19.2 12.5 %all-to-all-done.2 = bf16[2,128,16,128]{1,3,0,2:T(8,128)(2,1)S(1)} async-done(((bf16[2,128,16,128]{1,3,0,2:T(8,128)(2,1)}), bf16[2,128,16,128]{1,3,0,2:T(8,128)(2,1)S(1)}, u32[]{:S(2)}, u32[]{:S(2)}) %all-to-all-start.2) | async-done | bytes 1048608 | tf_op jit(solution)/shard_map/all_to_all | solution.py:81
  31.7 5.9 %all-to-all-start = ((bf16[2,128,16,128]{1,3,0,2:T(8,128)(2,1)}), bf16[2,128,16,128]{1,3,0,2:T(8,128)(2,1)S(1)}, u32[]{:S(2)}, u32[]{:S(2)}) async-start(bf16[2,128,16,128]{1,3,0,2:T(8,128)(2,1)} %copy.99), calls=%async_computation | async-start | bytes 2097152 | tf_op jit(solution)/shard_map/all_to_all | solution.py:79
  37.6 1.6 copy.102
  39.2 1.1 copy.103
  40.2 11.7 %all-to-all-done = bf16[2,128,16,128]{1,3,0,2:T(8,128)(2,1)S(1)} async-done(((bf16[2,128,16,128]{1,3,0,2:T(8,128)(2,1)}), bf16[2,128,16,128]{1,3,0,2:T(8,128)(2,1)S(1)}, u32[]{:S(2)}, u32[]{:S(2)}) %all-to-all-start) | async-done | bytes 1048608 | tf_op jit(solution)/shard_map/all_to_all | solution.py:79
  52.0 5.7 %all-to-all-start.1 = ((bf16[2,128,16,128]{1,3,0,2:T(8,128)(2,1)}), bf16[2,128,16,128]{1,3,0,2:T(8,128)(2,1)S(1)}, u32[]{:S(2)}, u32[]{:S(2)}) async-start(bf16[2,128,16,128]{1,3,0,2:T(8,128)(2,1)} %copy.103), calls=%async_computation.1 | async-start | bytes 2097152 | tf_op jit(solution)/shard_map/all_to_all | solution.py:80
  57.8 1.4 copy.109
  59.2 1.3 copy.101
  60.5 11.7 %all-to-all-done.1 = bf16[2,128,16,128]{1,3,0,2:T(8,128)(2,1)S(1)} async-done(((bf16[2,128,16,128]{1,3,0,2:T(8,128)(2,1)}), bf16[2,128,16,128]{1,3,0,2:T(8,128)(2,1)S(1)}, u32[]{:S(2)}, u32[]{:S(2)}) %all-to-all-start.1) | async-done | bytes 1048608 | tf_op jit(solution)/shard_map/all_to_all | solution.py:80
  72.1 0.7 copy.105
  72.8 11.3 %fusion.22 = (f32[2,2,1024]{2,1,0:T(2,128)S(1)}, bf16[2,2,1024,1024]{2,3,1,0:T(8,128)(2,1)}) fusion(pred[2,1024]{1,0:T(4,128)(4,1)S(1)} %get-tuple-element.11, bf16[2,1024,2,128]{3,1,2,0:T(8,128)(2,1)} %bitcast.70, bf16[2,1024,2,128]{3,1,2,0:T(8,128)(2,1)S(1)} %bitcast.71), kind=kOutput, calls=%fused_computation.50 | convolution fusion | flops 1098908672 | bytes 10504192 | tf_op jit(solution)/shard_map/sub | solution.py:92
  84.1 6.3 %fusion.13 = bf16[2,1024,2,128]{3,1,2,0:T(8,128)(2,1)S(1)} fusion(bf16[2,1024,2,128]{3,1,2,0:T(8,128)(2,1)S(1)} %bitcast.69, bf16[2,2,1024,1024]{2,3,1,0:T(8,128)(2,1)} %get-tuple-element.13, f32[2,1024,2]{1,2,0:T(2,128)S(1)} %bitcast.72), kind=kOutput, calls=%fused_computation.21 | convolution fusion | flops 1074790400 | bytes 10502144 | tf_op jit(solution)/shard_map/ehij,ejhd->eihd/dot_general | solution.py:94
  90.5 2.1 copy.111
  92.6 5.7 %all-to-all-start.3 = ((bf16[2,1024,2,128]{3,2,0,1:T(2,128)(2,1)}), bf16[2,1024,2,128]{3,2,0,1:T(2,128)(2,1)S(1)}, u32[]{:S(2)}, u32[]{:S(2)}) async-start(bf16[2,1024,2,128]{3,2,0,1:T(2,128)(2,1)} %copy.111), calls=%async_computation.3 | async-start | bytes 2097152 | tf_op jit(solution)/shard_map/all_to_all | solution.py:98
  98.3 0.6 convert_reduce_fusion.1
  99.0 0.7 pad_maximum_fusion
  99.7 13.0 %all-to-all-done.3 = bf16[2,1024,2,128]{3,2,0,1:T(2,128)(2,1)S(1)} async-done(((bf16[2,1024,2,128]{3,2,0,1:T(2,128)(2,1)}), bf16[2,1024,2,128]{3,2,0,1:T(2,128)(2,1)S(1)}, u32[]{:S(2)}, u32[]{:S(2)}) %all-to-all-start.3) | async-done | bytes 1048608 | tf_op jit(solution)/shard_map/all_to_all | solution.py:98
  112.7 0.6 broadcast_in_dim.33
  113.3 7.6 %all-to-all-start.7 = ((f32[16,1,13]{2,1,0:T(1,128)}), f32[16,1,13]{2,1,0:T(1,128)S(1)}, u32[]{:S(2)}, u32[]{:S(2)}) async-start(f32[16,1,13]{2,1,0:T(1,128)} %broadcast_in_dim.33), calls=%async_computation.7 | async-start | bytes 16384 | tf_op jit(solution)/shard_map/all_to_all | solution.py:21
  120.9 0.7 copy.128
  121.6 0.8 reshape_reshape.6
  122.4 6.1 %convolution_convert_fusion.1 = bf16[256,2176]{1,0:T(8,128)(2,1)S(1)} fusion(bf16[256,2048]{1,0:T(8,128)(2,1)S(1)} %reshape_reshape.6, bf16[2048,2176]{1,0:T(8,128)(2,1)} %param.16), kind=kOutput, calls=%fused_computation.19 | convolution fusion | flops 2282258432 | bytes 11075584 | tf_op jit(solution)/shard_map/dot_general | solution.py:121
  128.6 1.2 stack.3
  129.7 104.8 %all_to_all.95 = bf16[8,2,128,2176]{3,2,1,0:T(8,128)(2,1)} all-to-all(bf16[8,2,128,2176]{3,2,1,0:T(8,128)(2,1)S(1)} %stack.3), channel_id=1, replica_groups=mesh['cp'=8,'grp'=16] {'cp'}, dimensions={0} | all-to-all | bytes 17825792 | tf_op jit(solution)/shard_map/all_to_all | solution.py:128
  234.5 1.5 broadcast_in_dim.31
  236.1 6.9 %all-to-all-start.5 = ((bf16[16,136,512]{2,1,0:T(8,128)(2,1)}), bf16[16,136,512]{2,1,0:T(8,128)(2,1)S(1)}, u32[]{:S(2)}, u32[]{:S(2)}) async-start(bf16[16,136,512]{2,1,0:T(8,128)(2,1)} %broadcast_in_dim.31), calls=%async_computation.5 | async-start | bytes 4456448 | tf_op jit(solution)/shard_map/all_to_all | solution.py:21
  243.1 0.6 slice.15
  244.6 8.0 %copy.113 = bf16[8,2,128,2176]{3,2,0,1:T(8,128)(2,1)} copy(bf16[8,2,128,2176]{3,2,1,0:T(8,128)(2,1)} %all_to_all.95) | data formatting | bytes 17825792 | tf_op jit(solution)/shard_map/all_to_all | solution.py:128
  252.6 18.7 %all-to-all-done.5 = bf16[16,136,512]{2,1,0:T(8,128)(2,1)S(1)} async-done(((bf16[16,136,512]{2,1,0:T(8,128)(2,1)}), bf16[16,136,512]{2,1,0:T(8,128)(2,1)S(1)}, u32[]{:S(2)}, u32[]{:S(2)}) %all-to-all-start.5) | async-done | bytes 2228256 | tf_op jit(solution)/shard_map/all_to_all | solution.py:21
  271.3 9.1 %multiply_reduce_fusion = (f32[2,512]{1,0:T(2,128)S(1)}, f32[2,1024,512]{2,1,0:T(8,128)}) fusion(f32[2,1024]{1,0:T(2,128)S(1)} %get-tuple-element.10, bf16[2,1024,2176]{2,1,0:T(8,128)(2,1)} %bitcast.54, bf16[2176,512,1]{1,0,2:T(8,128)(2,1)S(1)} %bitcast.65), kind=kOutput, calls=%fused_computation.17 | convolution fusion | flops 4569693184 | bytes 15347712 | tf_op jit(solution)/shard_map/dot_general | solution.py:133
  280.7 0.7 broadcast_in_dim.32
  281.4 3.4 all-to-all-start.6
  285.0 6.7 %all-to-all-done.6 = f32[8,14,256]{2,1,0:T(8,128)S(1)} async-done(((f32[8,14,256]{2,1,0:T(8,128)}), f32[8,14,256]{2,1,0:T(8,128)S(1)}, u32[]{:S(2)}, u32[]{:S(2)}) %all-to-all-start.6) | async-done | bytes 114720 | tf_op jit(solution)/shard_map/all_to_all | solution.py:21
  291.8 0.2 exponential_reduce_fusion
  292.0 1.0 convolution_convert_fusion.2
  293.1 0.2 fusion.21
  293.3 4.0 %fusion.12 = bf16[2,1024,512]{2,1,0:T(8,128)(2,1)S(1)} fusion(f32[2,1024,512]{2,1,0:T(8,128)} %get-tuple-element.15, f32[2,512]{1,0:T(2,128)S(1)} %reduce_sum.154, f32[2,1024]{1,0:T(2,128)S(1)} %broadcast_divide_fusion), kind=kLoop, calls=%fused_computation.16 | loop fusion | flops 11534336 | bytes 6303744 | tf_op jit(solution)/shard_map/convert_element_type | solution.py:186
  297.3 9.8 %convolution_convert_fusion = bf16[2176,512]{1,0:T(8,128)(2,1)} fusion(bf16[2048,2176]{1,0:T(8,128)(2,1)} %bitcast.55, bf16[2048,512]{1,0:T(8,128)(2,1)S(1)} %bitcast.67), kind=kOutput, calls=%fused_computation.10 | convolution fusion | flops 4564516864 | bytes 13238272 | tf_op jit(solution)/shard_map/dot_general | solution.py:191
  307.2 5.6 %all-to-all-start.8 = ((bf16[16,136,512]{2,1,0:T(8,128)(2,1)}), bf16[16,136,512]{2,1,0:T(8,128)(2,1)S(1)}, u32[]{:S(2)}, u32[]{:S(2)}) async-start(bf16[16,136,512]{2,1,0:T(8,128)(2,1)} %bitcast.66), calls=%async_computation.8 | async-start | bytes 4456448 | tf_op jit(solution)/shard_map/all_to_all | solution.py:53
  313.0 0.6 reshape.158
  313.6 37.6 %all-to-all-done.8 = bf16[16,136,512]{2,1,0:T(8,128)(2,1)S(1)} async-done(((bf16[16,136,512]{2,1,0:T(8,128)(2,1)}), bf16[16,136,512]{2,1,0:T(8,128)(2,1)S(1)}, u32[]{:S(2)}, u32[]{:S(2)}) %all-to-all-start.8) | async-done | bytes 2228256 | tf_op jit(solution)/shard_map/all_to_all | solution.py:53
  351.3 1.0 reduce_sum.155
  352.3 3.5 reduce_sum.156
  (46 shorter events, 1.5 us)
Async XLA Ops:
  7.2 273.4 %copy-start = (bf16[512,256]{1,0:T(8,128)(2,1)S(1)}, bf16[512,256]{1,0:T(8,128)(2,1)}, u32[]{:S(2)}) copy-start(bf16[512,256]{1,0:T(8,128)(2,1)} %param.18) | copy-start | bytes 786436
  7.2 10.3 %copy-start.1 = (bf16[2,128,2048]{2,1,0:T(8,128)(2,1)S(1)}, bf16[2,128,2048]{2,1,0:T(8,128)(2,1)}, u32[]{:S(2)}) copy-start(bf16[2,128,2048]{2,1,0:T(8,128)(2,1)} %param.12) | copy-start | bytes 3145732
  10.0 21.7 %all-to-all-start.2 = ((bf16[2,128,16,128]{1,3,0,2:T(8,128)(2,1)}), bf16[2,128,16,128]{1,3,0,2:T(8,128)(2,1)S(1)}, u32[]{:S(2)}, u32[]{:S(2)}) async-start(bf16[2,128,16,128]{1,3,0,2:T(8,128)(2,1)} %copy.107), calls=%async_computation.2 | async-start | bytes 2097152 | tf_op jit(solution)/shard_map/all_to_all | solution.py:81
  19.2 38.5 %copy-start.5 = (s32[2]{0:T(128)S(1)}, s32[2]{0:T(128)}, u32[]{:S(2)}) copy-start(s32[2]{0:T(128)} %param.15) | copy-start | bytes 28
  31.7 20.3 %all-to-all-start = ((bf16[2,128,16,128]{1,3,0,2:T(8,128)(2,1)}), bf16[2,128,16,128]{1,3,0,2:T(8,128)(2,1)S(1)}, u32[]{:S(2)}, u32[]{:S(2)}) async-start(bf16[2,128,16,128]{1,3,0,2:T(8,128)(2,1)} %copy.99), calls=%async_computation | async-start | bytes 2097152 | tf_op jit(solution)/shard_map/all_to_all | solution.py:79
  52.0 20.1 %all-to-all-start.1 = ((bf16[2,128,16,128]{1,3,0,2:T(8,128)(2,1)}), bf16[2,128,16,128]{1,3,0,2:T(8,128)(2,1)S(1)}, u32[]{:S(2)}, u32[]{:S(2)}) async-start(bf16[2,128,16,128]{1,3,0,2:T(8,128)(2,1)} %copy.103), calls=%async_computation.1 | async-start | bytes 2097152 | tf_op jit(solution)/shard_map/all_to_all | solution.py:80
  72.8 11.4 %copy-start.2 = (bf16[2,8,128,2,128]{4,2,1,3,0:T(8,128)(2,1)S(1)}, bf16[2,8,128,2,128]{4,2,1,3,0:T(8,128)(2,1)}, u32[]{:S(2)}) copy-start(bf16[2,8,128,2,128]{4,2,1,3,0:T(8,128)(2,1)} %copy.109) | copy-start | bytes 3145732
  90.5 7.8 %copy-start.7 = (f32[2]{0:T(128)S(1)}, f32[2]{0:T(128)}, u32[]{:S(2)}) copy-start(f32[2]{0:T(128)} %param.23) | copy-start | bytes 28
  90.5 7.8 %copy-start.8 = (s32[2,7]{1,0:T(2,128)S(1)}, s32[2,7]{1,0:T(2,128)}, u32[]{:S(2)}) copy-start(s32[2,7]{1,0:T(2,128)} %param.21) | copy-start | bytes 172
  90.5 8.4 %copy-start.6 = (s32[2]{0:T(128)S(1)}, s32[2]{0:T(128)}, u32[]{:S(2)}) copy-start(s32[2]{0:T(128)} %param.22) | copy-start | bytes 28
  92.6 20.1 %all-to-all-start.3 = ((bf16[2,1024,2,128]{3,2,0,1:T(2,128)(2,1)}), bf16[2,1024,2,128]{3,2,0,1:T(2,128)(2,1)S(1)}, u32[]{:S(2)}, u32[]{:S(2)}) async-start(bf16[2,1024,2,128]{3,2,0,1:T(2,128)(2,1)} %copy.111), calls=%async_computation.3 | async-start | bytes 2097152 | tf_op jit(solution)/shard_map/all_to_all | solution.py:98
  113.3 15.3 %all-to-all-start.7 = ((f32[16,1,13]{2,1,0:T(1,128)}), f32[16,1,13]{2,1,0:T(1,128)S(1)}, u32[]{:S(2)}, u32[]{:S(2)}) async-start(f32[16,1,13]{2,1,0:T(1,128)} %broadcast_in_dim.33), calls=%async_computation.7 | async-start | bytes 16384 | tf_op jit(solution)/shard_map/all_to_all | solution.py:21
  129.7 104.8 %copy-start.3 = (bf16[136,512]{1,0:T(8,128)(2,1)S(1)}, bf16[136,512]{1,0:T(8,128)(2,1)}, u32[]{:S(2)}) copy-start(bf16[136,512]{1,0:T(8,128)(2,1)} %param.17) | copy-start | bytes 417796
  234.5 8.4 %copy-start.9 = (s32[2,7]{1,0:T(2,128)S(1)}, s32[2,7]{1,0:T(2,128)}, u32[]{:S(2)}) copy-start(s32[2,7]{1,0:T(2,128)} %param.20) | copy-start | bytes 172
  236.1 35.3 %all-to-all-start.5 = ((bf16[16,136,512]{2,1,0:T(8,128)(2,1)}), bf16[16,136,512]{2,1,0:T(8,128)(2,1)S(1)}, u32[]{:S(2)}, u32[]{:S(2)}) async-start(bf16[16,136,512]{2,1,0:T(8,128)(2,1)} %broadcast_in_dim.31), calls=%async_computation.5 | async-start | bytes 4456448 | tf_op jit(solution)/shard_map/all_to_all | solution.py:21
  271.3 9.2 %copy-start.4 = (f32[7,512]{1,0:T(8,128)S(1)}, f32[7,512]{1,0:T(8,128)}, u32[]{:S(2)}) copy-start(f32[7,512]{1,0:T(8,128)} %param.19) | copy-start | bytes 43012
  281.4 10.3 %all-to-all-start.6 = ((f32[8,14,256]{2,1,0:T(8,128)}), f32[8,14,256]{2,1,0:T(8,128)S(1)}, u32[]{:S(2)}, u32[]{:S(2)}) async-start(f32[8,14,256]{2,1,0:T(8,128)} %broadcast_in_dim.32), calls=%async_computation.6 | async-start | bytes 262144 | tf_op jit(solution)/shard_map/all_to_all | solution.py:21
  284.8 67.5 %all-gather.3.cloned.1.call-start = ((), (), s32[]{:S(2)}) async-start(), calls=%async_computation.9 | async-start | bytes 4456448 | tf_op jit(solution)/shard_map/all_gather | solution.py:42
  307.2 44.1 %all-to-all-start.8 = ((bf16[16,136,512]{2,1,0:T(8,128)(2,1)}), bf16[16,136,512]{2,1,0:T(8,128)(2,1)S(1)}, u32[]{:S(2)}, u32[]{:S(2)}) async-start(bf16[16,136,512]{2,1,0:T(8,128)(2,1)} %bitcast.66), calls=%async_computation.8 | async-start | bytes 4456448 | tf_op jit(solution)/shard_map/all_to_all | solution.py:53
Sparse Core Ops, SparseCore 0:
  293.1 57.2 all-gather.2
